TPU v7x, 32 devices: a whole 2x2x4 slice. The times are simulated.
32 devices in a mesh: dp: 8 (over z, core), seq: 4 (over y, x).
Axes of the slice: x: 2, y: 2, z: 4, core: 2. Of those that a mesh axis runs over, the one named last changes fastest.
Arguments:
- tokens: bfloat16 [1024, 4096], P(('dp', 'seq')), may hold values from -6 to 6
- modality: int32 [1024], P(('dp', 'seq')), may hold values from 0 to 1, as said below
- gate_weight: bfloat16 [4096, 14336], P(None, 'dp'), may hold values from -0.09375 to 0.09375
- up_weight: bfloat16 [4096, 14336], P(None, 'dp'), may hold values from -0.09375 to 0.09375
- down_weight: bfloat16 [14336, 4096], P('dp'), may hold values from -0.046875 to 0.046875
- out_grad: bfloat16 [768, 4096], P(('dp', 'seq')), may hold values from -1.5 to 1.5
Outputs:
- output: bfloat16 [768, 4096], P(('dp', 'seq'))
- in_grad: bfloat16 [768, 4096], P(('dp', 'seq'))
- gate_grad: bfloat16 [4096, 14336], P('seq', 'dp')
- up_grad: bfloat16 [4096, 14336], P('seq', 'dp')
- down_grad: bfloat16 [14336, 4096], P('dp', 'seq')
Inputs may be any that keep to these rules, and one draw needn't show every extreme that they name: In each aligned block of 32 tokens (the tokens of one device) exactly 24 tokens have modality 1 (vision); all others have 0 (text).
All inputs are finite; a program needn't handle non-finite values.
Results may differ from a plain program's by a relative error of at most 0.014.
Values may be sent and summed in bfloat16 or wider, within the bound.
No kernel may reach another device: no remote copies, remote signals or barrier semaphores. Data moves between devices by JAX's collectives and lax.ppermute only.
A program may use at most 192 MiB of HBM per device.

v0:
```python
import jax
import jax.numpy as jnp
from jax import lax
from jax.sharding import PartitionSpec as P


def silu_parts(gate_proj):
    sigmoid_value = jax.nn.sigmoid(gate_proj)
    return (gate_proj * sigmoid_value, sigmoid_value * (1.0 + gate_proj * (1.0 - sigmoid_value)))


def contract_cols(left_matrix, right_matrix):
    return lax.dot_general(
        left_matrix, right_matrix, (((1,), (1,)), ((), ())), preferred_element_type=jnp.float32
    )


def group_sum(left_blocks, right_blocks, form):
    partials = jnp.einsum(
        form, left_blocks, right_blocks, preferred_element_type=jnp.float32
    ).astype(jnp.bfloat16)
    partials = lax.optimization_barrier(partials)
    return jnp.sum(partials.astype(jnp.float32), axis=0)


def on_device(tokens, modality, gate_weight, up_weight, down_weight, out_grad):
    vision_count = out_grad.shape[0]
    flags = (modality == 1).astype(jnp.int32)
    ranks = jnp.cumsum(flags) - 1
    slot_ids = jnp.arange(vision_count, dtype=jnp.int32)[:, None]
    selector = ((ranks[None, :] == slot_ids) & (flags[None, :] == 1)).astype(jnp.bfloat16)
    picked = jnp.dot(selector, tokens, preferred_element_type=jnp.float32).astype(jnp.bfloat16)
    token_rows = lax.all_gather(picked, "dp", axis=0, tiled=True)
    gate_proj = jnp.dot(token_rows, gate_weight, preferred_element_type=jnp.float32)
    up_proj = jnp.dot(token_rows, up_weight, preferred_element_type=jnp.float32)
    active, slope = silu_parts(gate_proj)
    hidden = (active * up_proj).astype(jnp.bfloat16)
    output = lax.psum_scatter(
        jnp.dot(hidden, down_weight, preferred_element_type=jnp.float32).astype(jnp.bfloat16),
        "dp",
        scatter_dimension=0,
        tiled=True,
    )
    cotangent_rows = lax.all_gather(out_grad, "dp", axis=0, tiled=True)
    back_hidden = contract_cols(cotangent_rows, down_weight)
    gate_back = (back_hidden * up_proj * slope).astype(jnp.bfloat16)
    up_back = (back_hidden * active).astype(jnp.bfloat16)
    in_grad = lax.psum_scatter(
        (contract_cols(gate_back, gate_weight) + contract_cols(up_back, up_weight)).astype(
            jnp.bfloat16
        ),
        "dp",
        scatter_dimension=0,
        tiled=True,
    )
    group_count = lax.axis_size("seq")
    row_total = token_rows.shape[0]
    split_tokens, split_cotangent = (
        lax.all_to_all(token_rows, "seq", split_axis=1, concat_axis=0, tiled=True),
        lax.all_to_all(cotangent_rows, "seq", split_axis=1, concat_axis=0, tiled=True),
    )
    all_hidden, all_gate_back, all_up_back = (
        lax.all_gather(hidden, "seq", axis=0, tiled=True),
        lax.all_gather(gate_back, "seq", axis=0, tiled=True),
        lax.all_gather(up_back, "seq", axis=0, tiled=True),
    )

    def per_group(matrix):
        return matrix.reshape(group_count, row_total, matrix.shape[1])

    gate_total = group_sum(per_group(split_tokens), per_group(all_gate_back), "jrd,jrf->jdf")
    up_total = group_sum(per_group(split_tokens), per_group(all_up_back), "jrd,jrf->jdf")
    down_total = group_sum(per_group(all_hidden), per_group(split_cotangent), "jrf,jrd->jfd")
    return (
        output,
        in_grad,
        gate_total.astype(jnp.bfloat16),
        up_total.astype(jnp.bfloat16),
        down_total.astype(jnp.bfloat16),
    )


def solution(mesh):
    placed = (
        P(("dp", "seq"), None),
        P(("dp", "seq")),
        P(None, "dp"),
        P(None, "dp"),
        P("dp", None),
        P(("dp", "seq"), None),
    )
    return jax.shard_map(
        on_device,
        mesh=mesh,
        in_specs=placed,
        out_specs=(
            P(("dp", "seq"), None),
            P(("dp", "seq"), None),
            P("seq", "dp"),
            P("seq", "dp"),
            P("dp", "seq"),
        ),
        check_vma=False,
    )
```

profile of v0, /device:TPU:0, one launch (start us, length us, event | category | flops | bytes accessed | tf_op | source)
XLA Modules:
  0.0 296.2 jit_solution(6966429705825907858)
XLA Ops:
  7.2 0.7 fusion.9
  7.9 0.1 copy.13
  8.0 0.1 reduce-window.8
  8.1 0.1 add_reduce_fusion
  8.2 0.9 convolution_convert_fusion.4
  9.1 0.7 all-gather.8.cloned.1.call-update
  9.9 28.3 %all-gather.6.cloned.1.call-done = bf16[192,4096]{1,0:T(8,128)(2,1)} async-done(((bf16[24,4096]{1,0:T(8,128)(2,1)}), bf16[192,4096]{1,0:T(8,128)(2,1)}) %all-gather.6.cloned.1.call-update) | async-done | bytes 1572880 | tf_op jit(solution)/shard_map/all_gather | solution.py:33
  38.2 9.3 %fusion.12 = f32[192,1792]{1,0:T(8,128)S(1)} fusion(bf16[192,4096]{1,0:T(8,128)(2,1)} %all-gather.6.cloned.1.call-done, bf16[4096,1792]{1,0:T(8,128)(2,1)} %param.9), kind=kOutput, calls=%fused_computation.26 | convolution fusion | flops 2818572288 | bytes 17629184 | tf_op jit(solution)/shard_map/dot_general | solution.py:35
  47.5 1.3 copy-done.5
  48.8 4.2 %fusion.11 = f32[192,1792]{1,0:T(8,128)} fusion(bf16[192,4096]{1,0:T(8,128)(2,1)S(1)} %copy-done.2, bf16[4096,1792]{1,0:T(8,128)(2,1)S(1)} %copy-done.5), kind=kOutput, calls=%fused_computation.25 | convolution fusion | flops 2818572288 | bytes 17629184 | tf_op jit(solution)/shard_map/dot_general | solution.py:34
  53.0 11.3 %all-gather.8.cloned.1.call-done = bf16[192,4096]{1,0:T(8,128)(2,1)} async-done(((bf16[24,4096]{1,0:T(8,128)(2,1)}), bf16[192,4096]{1,0:T(8,128)(2,1)}) %all-gather.8.cloned.1.call-update) | async-done | bytes 1572880 | tf_op jit(solution)/shard_map/all_gather | solution.py:44
  64.3 12.5 %multiply_convert_fusion = (bf16[192,1792]{1,0:T(8,128)(2,1)}, bf16[192,1792]{1,0:T(8,128)(2,1)}, bf16[192,1792]{1,0:T(8,128)(2,1)}) fusion(f32[192,1792]{1,0:T(8,128)} %fusion.11, f32[192,1792]{1,0:T(8,128)S(1)} %fusion.12, bf16[192,4096]{1,0:T(8,128)(2,1)} %all-gather.8.cloned.1.call-done, bf16[1792,4096]{1,0:T(8,128)(2,1)} %param.10), kind=kOutput, calls=%fused_computation.12 | convolution fusion | flops 2823733248 | bytes 21069824 | tf_op jit(solution)/shard_map/dot_general | solution.py:13
  76.9 0.5 all-gather.12.cloned.1.call-update
  77.5 0.5 all-gather.10.cloned.1.call-update
  78.1 9.9 %convolution_convert_fusion.3 = bf16[192,4096]{1,0:T(8,128)(2,1)} fusion(bf16[192,1792]{1,0:T(8,128)(2,1)} %get-tuple-element.7, bf16[1792,4096]{1,0:T(8,128)(2,1)} %param.10), kind=kOutput, calls=%fused_computation.5 | convolution fusion | flops 2819358720 | bytes 16941056 | tf_op jit(solution)/shard_map/dot_general | solution.py:39
  88.0 1.3 copy.20
  89.3 3.7 %all-to-all-start.1 = ((bf16[192,4,1024]{2,0,1:T(8,128)(2,1)}), bf16[192,4,1024]{2,0,1:T(8,128)(2,1)S(1)}, u32[]{:S(2)}, u32[]{:S(2)}) async-start(bf16[192,4,1024]{2,0,1:T(8,128)(2,1)} %bitcast.35), calls=%async_computation.3 | async-start | bytes 3145728 | tf_op jit(solution)/shard_map/all_to_all | solution.py:60
  93.1 1.3 copy.21
  94.4 11.7 %fusion.13 = f32[192,4096]{1,0:T(8,128)} fusion(bf16[192,1792]{1,0:T(8,128)(2,1)S(1)} %copy-done.4, bf16[4096,1792]{1,0:T(8,128)(2,1)} %param.8), kind=kOutput, calls=%fused_computation.27 | convolution fusion | flops 2818572288 | bytes 18513920 | tf_op jit(solution)/shard_map/dot_general | solution.py:13
  106.1 18.2 %all-to-all-done.1 = bf16[192,4,1024]{2,0,1:T(8,128)(2,1)S(1)} async-done(((bf16[192,4,1024]{2,0,1:T(8,128)(2,1)}), bf16[192,4,1024]{2,0,1:T(8,128)(2,1)S(1)}, u32[]{:S(2)}, u32[]{:S(2)}) %all-to-all-start.1) | async-done | bytes 1572896 | tf_op jit(solution)/shard_map/all_to_all | solution.py:60
  124.3 3.6 %all-to-all-start = ((bf16[192,4,1024]{2,0,1:T(8,128)(2,1)}), bf16[192,4,1024]{2,0,1:T(8,128)(2,1)S(1)}, u32[]{:S(2)}, u32[]{:S(2)}) async-start(bf16[192,4,1024]{2,0,1:T(8,128)(2,1)} %bitcast.37), calls=%async_computation.2 | async-start | bytes 3145728 | tf_op jit(solution)/shard_map/all_to_all | solution.py:59
  127.9 12.3 %fusion = bf16[192,4096]{1,0:T(8,128)(2,1)} fusion(f32[192,4096]{1,0:T(8,128)} %fusion.13, bf16[192,1792]{1,0:T(8,128)(2,1)} %get-tuple-element.5, bf16[4096,1792]{1,0:T(8,128)(2,1)} %param.9), kind=kOutput, calls=%fused_computation.4 | convolution fusion | flops 2820145152 | bytes 20086784 | tf_op jit(solution)/shard_map/dot_general | solution.py:13
  140.3 9.5 %convolution_convert_fusion = bf16[4,1792,1024]{2,1,0:T(8,128)(2,1)} fusion(bf16[4,192,1792]{2,1,0:T(8,128)(2,1)} %bitcast.40, bf16[192,4,1024]{2,0,1:T(8,128)(2,1)S(1)} %all-to-all-done.1), kind=kOutput, calls=%fused_computation | convolution fusion | flops 2825912320 | bytes 19005440 | tf_op jit(solution)/shard_map/jrf,jrd->jfd/dot_general | solution.py:19
  149.8 24.9 %all-gather.12.cloned.1.call-done = bf16[768,1792]{1,0:T(8,128)(2,1)} async-done(((bf16[192,1792]{1,0:T(8,128)(2,1)}), bf16[768,1792]{1,0:T(8,128)(2,1)}) %all-gather.12.cloned.1.call-update) | async-done | bytes 2752528 | tf_op jit(solution)/shard_map/all_gather | solution.py:65
  174.7 9.2 %convolution_convert_fusion.1 = bf16[4,1024,1792]{2,1,0:T(8,128)(2,1)} fusion(bf16[4,192,1792]{2,1,0:T(8,128)(2,1)} %bitcast.38, bf16[192,4,1024]{2,0,1:T(8,128)(2,1)S(1)} %all-to-all-done), kind=kOutput, calls=%fused_computation.1 | convolution fusion | flops 2825912320 | bytes 19005440 | tf_op jit(solution)/shard_map/jrd,jrf->jdf/dot_general | solution.py:19
  183.9 11.1 %reduce_sum.38 = bf16[1792,1024]{1,0:T(8,128)(2,1)} reduce(bf16[4,1792,1024]{2,1,0:T(8,128)(2,1)} %convolution_convert_fusion, bf16[]{:T(256)} %constant.15.clone.1), dimensions={0}, to_apply=%region_5.6 | reduce | flops 5505024 | bytes 18350082 | tf_op jit(solution)/shard_map/reduce_sum | solution.py:23
  195.1 10.9 %reduce_sum.37 = bf16[1024,1792]{1,0:T(8,128)(2,1)} reduce(bf16[4,1024,1792]{2,1,0:T(8,128)(2,1)} %convolution_convert_fusion.1, bf16[]{:T(256)} %constant.15.clone.1), dimensions={0}, to_apply=%region_4.5 | reduce | flops 5505024 | bytes 18350082 | tf_op jit(solution)/shard_map/reduce_sum | solution.py:23
  206.0 11.0 %all-gather.10.cloned.1.call-done = bf16[768,1792]{1,0:T(8,128)(2,1)} async-done(((bf16[192,1792]{1,0:T(8,128)(2,1)}), bf16[768,1792]{1,0:T(8,128)(2,1)}) %all-gather.10.cloned.1.call-update) | async-done | bytes 2752528 | tf_op jit(solution)/shard_map/all_gather | solution.py:64
  217.0 9.2 %convolution_convert_fusion.2 = bf16[4,1024,1792]{2,1,0:T(8,128)(2,1)} fusion(bf16[4,192,1792]{2,1,0:T(8,128)(2,1)} %bitcast.39, bf16[192,4,1024]{2,0,1:T(8,128)(2,1)S(1)} %all-to-all-done), kind=kOutput, calls=%fused_computation.2 | convolution fusion | flops 2825912320 | bytes 19005440 | tf_op jit(solution)/shard_map/jrd,jrf->jdf/dot_general | solution.py:19
  226.2 10.7 %reduce_sum.36 = bf16[1024,1792]{1,0:T(8,128)(2,1)} reduce(bf16[4,1024,1792]{2,1,0:T(8,128)(2,1)} %convolution_convert_fusion.2, bf16[]{:T(256)} %constant.15.clone.1), dimensions={0}, to_apply=%region_3.4 | reduce | flops 5505024 | bytes 18350082 | tf_op jit(solution)/shard_map/reduce_sum | solution.py:23
  237.0 16.9 %reduce-scatter.3.cloned.1.call-done = bf16[24,4096]{1,0:T(8,128)(2,1)} async-done(((bf16[192,4096]{1,0:T(8,128)(2,1)}), bf16[24,4096]{1,0:T(8,128)(2,1)}) %reduce-scatter.3.cloned.1.call-update) | async-done | bytes 196624 | tf_op jit(solution)/shard_map/reduce_scatter | solution.py:38
  253.9 35.5 %reduce-scatter.5.cloned.1.call-done = bf16[24,4096]{1,0:T(8,128)(2,1)} async-done(((bf16[192,4096]{1,0:T(8,128)(2,1)}), bf16[24,4096]{1,0:T(8,128)(2,1)}) %reduce-scatter.5.cloned.1.call-update) | async-done | bytes 196624 | tf_op jit(solution)/shard_map/reduce_scatter | solution.py:48
  (24 shorter events, 0.4 us)
Async XLA Ops:
  7.2 1.0 copy-start
  7.2 31.0 %all-gather.6.cloned.1.call-start = ((), (), s32[]{:S(2)}) async-start(), calls=%async_computation.4 | async-start | bytes 1769472 | tf_op jit(solution)/shard_map/all_gather | solution.py:33
  9.1 55.2 %all-gather.8.cloned.1.call-start = ((), (), s32[]{:S(2)}) async-start(), calls=%async_computation.6 | async-start | bytes 1769472 | tf_op jit(solution)/shard_map/all_gather | solution.py:44
  9.8 130.4 %all-gather.14.cloned.1.call-start = ((), (), s32[]{:S(2)}) async-start(), calls=%async_computation.10 | async-start | bytes 3440640 | tf_op jit(solution)/shard_map/all_gather | solution.py:63
  38.2 9.3 %copy-start.2 = (bf16[192,4096]{1,0:T(8,128)(2,1)S(1)}, bf16[192,4096]{1,0:T(8,128)(2,1)}, u32[]{:S(2)}) copy-start(bf16[192,4096]{1,0:T(8,128)(2,1)} %all-gather.6.cloned.1.call-done) | copy-start | bytes 4718596
  38.2 10.6 %copy-start.5 = (bf16[4096,1792]{1,0:T(8,128)(2,1)S(1)}, bf16[4096,1792]{1,0:T(8,128)(2,1)}, u32[]{:S(2)}) copy-start(bf16[4096,1792]{1,0:T(8,128)(2,1)} %param.8) | copy-start | bytes 44040196
  76.8 97.8 %all-gather.12.cloned.1.call-start = ((), (), s32[]{:S(2)}) async-start(), calls=%async_computation.9 | async-start | bytes 3440640 | tf_op jit(solution)/shard_map/all_gather | solution.py:65
  77.4 139.6 %all-gather.10.cloned.1.call-start = ((), (), s32[]{:S(2)}) async-start(), calls=%async_computation.8 | async-start | bytes 3440640 | tf_op jit(solution)/shard_map/all_gather | solution.py:64
  78.0 10.0 %copy-start.3 = (bf16[192,4096]{1,0:T(8,128)(2,1)S(1)}, bf16[192,4096]{1,0:T(8,128)(2,1)}, u32[]{:S(2)}) copy-start(bf16[192,4096]{1,0:T(8,128)(2,1)} %all-gather.8.cloned.1.call-done) | copy-start | bytes 4718596
  78.0 175.8 %reduce-scatter.3.cloned.1.call-start = ((), (), s32[]{:S(2)}) async-start(), calls=%async_computation.5 | async-start | bytes 1769472 | tf_op jit(solution)/shard_map/reduce_scatter | solution.py:38
  89.3 34.9 %all-to-all-start.1 = ((bf16[192,4,1024]{2,0,1:T(8,128)(2,1)}), bf16[192,4,1024]{2,0,1:T(8,128)(2,1)S(1)}, u32[]{:S(2)}, u32[]{:S(2)}) async-start(bf16[192,4,1024]{2,0,1:T(8,128)(2,1)} %bitcast.35), calls=%async_computation.3 | async-start | bytes 3145728 | tf_op jit(solution)/shard_map/all_to_all | solution.py:60
  93.1 1.3 copy-start.4
  124.3 25.5 %all-to-all-start = ((bf16[192,4,1024]{2,0,1:T(8,128)(2,1)}), bf16[192,4,1024]{2,0,1:T(8,128)(2,1)S(1)}, u32[]{:S(2)}, u32[]{:S(2)}) async-start(bf16[192,4,1024]{2,0,1:T(8,128)(2,1)} %bitcast.37), calls=%async_computation.2 | async-start | bytes 3145728 | tf_op jit(solution)/shard_map/all_to_all | solution.py:59
  127.8 161.5 %reduce-scatter.5.cloned.1.call-start = ((), (), s32[]{:S(2)}) async-start(), calls=%async_computation.7 | async-start | bytes 1769472 | tf_op jit(solution)/shard_map/reduce_scatter | solution.py:48
  226.2 63.1 %copy-start.1 = (bf16[32,4096]{1,0:T(8,128)(2,1)S(1)}, bf16[32,4096]{1,0:T(8,128)(2,1)}, u32[]{:S(2)}) copy-start(bf16[32,4096]{1,0:T(8,128)(2,1)} %param.6) | copy-start | bytes 786436
Sparse Core Ops, SparseCore 0:
  10.2 27.9 all-gather.5
  39.9 24.3 all-gather.7
  77.0 50.7 all-gather.13
  129.4 45.1 all-gather.11
  176.4 40.5 all-gather.9
  219.7 34.0 reduce-scatter.2
  256.7 32.5 reduce-scatter.4
where the time goes:
time: 297 us; the launch traced here: 296 us
  waiting for transfers between devices  148 us (50%)
  matrix products  88.8 us (30%)
  other arithmetic  33.7 us (11%)
  between operations  14.2 us (5%)
  starting transfers between devices  7.58 us (3%)
  local copies, waits for them, and re-layouts  3.98 us (1%)
    dot_general x3, matrix products, contract_cols(): lax.dot_general(left_matrix, right_matrix, (((1,), (1,)), ((), ())), pref...  36.6 us
    reduce_scatter x1, waiting for transfers between devices, on_device(): lax.psum_scatter((contract_cols(gate_back, gate_weight) + contract_cols(u...  35.5 us
    reduce_sum x3, other arithmetic, group_sum(): return jnp.sum(partials.astype(jnp.float32), axis=0)  32.8 us
    all_gather x1, waiting for transfers between devices, on_device(): token_rows = lax.all_gather(picked, 'dp', axis=0, tiled=True)  28.3 us
    dot_general x3, matrix products, group_sum(): jnp.einsum(form, left_blocks, right_blocks, preferred_element_type=jnp.fl...  28 us
    all_gather x1, waiting for transfers between devices, on_device(): lax.all_gather(up_back, 'seq', axis=0, tiled=True)  24.9 us
    all_to_all x1, waiting for transfers between devices, on_device(): lax.all_to_all(cotangent_rows, 'seq', split_axis=1, concat_axis=0, tiled=...  18.2 us
    reduce_scatter x1, waiting for transfers between devices, on_device(): lax.psum_scatter(jnp.dot(hidden, down_weight, preferred_element_type=jnp....  16.9 us
  transfers between devices with their start and end apart: 9, of which 7 were waited for; matrix products, arithmetic and copies ran while one was open for 37% of the time, Pallas kernels for 0%

commit v1 on v0

--- a/solution.py
+++ b/solution.py
@@ -57,7 +57,12 @@
     row_total = token_rows.shape[0]
     split_tokens, split_cotangent = (
         lax.all_to_all(token_rows, "seq", split_axis=1, concat_axis=0, tiled=True),
-        lax.all_to_all(cotangent_rows, "seq", split_axis=1, concat_axis=0, tiled=True),
+        jnp.concatenate(
+            lax.all_to_all(
+                jnp.stack(jnp.split(cotangent_rows, lax.axis_size("seq"), axis=1)), "seq", 0, 0
+            ),
+            axis=0,
+        ),
     )
     all_hidden, all_gate_back, all_up_back = (
         lax.all_gather(hidden, "seq", axis=0, tiled=True),

time: 297 us -> 297 us (level)
    all_gather x1, waiting for transfers between devices: 24.9 us -> 19.8 us  [on_device(): lax.all_gather(up_back, 'seq', axis=0, tiled=True)]
  transfers between devices with their start and end apart: 9 -> 9, of which waited for: 7 -> 8; matrix products, arithmetic and copies ran while one was open for 37% -> 37% of each run, Pallas kernels for 0% -> 0%
where the time goes in v1:
time: 297 us
  waiting for transfers between devices  147 us (49%)
  matrix products  89 us (30%)
  other arithmetic  35 us (12%)
  between operations  14.2 us (5%)
  starting transfers between devices  7.58 us (3%)
  local copies, waits for them, and re-layouts  4.2 us (1%)
    dot_general x3, matrix products, contract_cols(): lax.dot_general(left_matrix, right_matrix, (((1,), (1,)), ((), ())), pref...  37.5 us
    reduce_scatter x1, waiting for transfers between devices, on_device(): lax.psum_scatter((contract_cols(gate_back, gate_weight) + contract_cols(u...  35.5 us
    reduce_sum x3, other arithmetic, group_sum(): return jnp.sum(partials.astype(jnp.float32), axis=0)  32.8 us
    all_gather x1, waiting for transfers between devices, on_device(): token_rows = lax.all_gather(picked, 'dp', axis=0, tiled=True)  28.3 us
    dot_general x3, matrix products, group_sum(): jnp.einsum(form, left_blocks, right_blocks, preferred_element_type=jnp.fl...  27.6 us
    all_gather x1, waiting for transfers between devices, on_device(): lax.all_gather(up_back, 'seq', axis=0, tiled=True)  19.8 us
    all_to_all x1, waiting for transfers between devices, on_device(): lax.all_to_all(jnp.stack(jnp.split(cotangent_rows, lax.axis_size('seq'),...  19.1 us
    reduce_scatter x1, waiting for transfers between devices, on_device(): lax.psum_scatter(jnp.dot(hidden, down_weight, preferred_element_type=jnp....  17 us
  transfers between devices with their start and end apart: 9, of which 8 were waited for; matrix products, arithmetic and copies ran while one was open for 37% of the time, Pallas kernels for 0%

profile of v1, /device:TPU:0, one launch (start us, length us, event | category | flops | bytes accessed | tf_op | source)
XLA Modules:
  0.0 296.6 jit_solution(4974576974688191667)
XLA Ops:
  7.2 0.7 fusion.8
  8.2 0.9 convolution_convert_fusion.4
  9.1 0.7 all-gather.8.cloned.1.call-update
  9.9 28.3 %all-gather.6.cloned.1.call-done = bf16[192,4096]{1,0:T(8,128)(2,1)} async-done(((bf16[24,4096]{1,0:T(8,128)(2,1)}), bf16[192,4096]{1,0:T(8,128)(2,1)}) %all-gather.6.cloned.1.call-update) | async-done | bytes 1572880 | tf_op jit(solution)/shard_map/all_gather | solution.py:33
  38.2 9.3 %fusion.11 = f32[192,1792]{1,0:T(8,128)S(1)} fusion(bf16[192,4096]{1,0:T(8,128)(2,1)} %all-gather.6.cloned.1.call-done, bf16[4096,1792]{1,0:T(8,128)(2,1)} %param.9), kind=kOutput, calls=%fused_computation.29 | convolution fusion | flops 2818572288 | bytes 17629184 | tf_op jit(solution)/shard_map/dot_general | solution.py:35
  47.5 1.3 copy-done.6
  48.8 4.2 %fusion.10 = f32[192,1792]{1,0:T(8,128)} fusion(bf16[192,4096]{1,0:T(8,128)(2,1)S(1)} %copy-done.2, bf16[4096,1792]{1,0:T(8,128)(2,1)S(1)} %copy-done.6), kind=kOutput, calls=%fused_computation.28 | convolution fusion | flops 2818572288 | bytes 17629184 | tf_op jit(solution)/shard_map/dot_general | solution.py:34
  53.0 11.3 %all-gather.8.cloned.1.call-done = bf16[192,4096]{1,0:T(8,128)(2,1)} async-done(((bf16[24,4096]{1,0:T(8,128)(2,1)}), bf16[192,4096]{1,0:T(8,128)(2,1)}) %all-gather.8.cloned.1.call-update) | async-done | bytes 1572880 | tf_op jit(solution)/shard_map/all_gather | solution.py:44
  64.3 12.5 %multiply_convert_fusion = (bf16[192,1792]{1,0:T(8,128)(2,1)}, bf16[192,1792]{1,0:T(8,128)(2,1)}, bf16[192,1792]{1,0:T(8,128)(2,1)}) fusion(f32[192,1792]{1,0:T(8,128)} %fusion.10, f32[192,1792]{1,0:T(8,128)S(1)} %fusion.11, bf16[192,4096]{1,0:T(8,128)(2,1)} %all-gather.8.cloned.1.call-done, bf16[1792,4096]{1,0:T(8,128)(2,1)} %param.10), kind=kOutput, calls=%fused_computation.11 | convolution fusion | flops 2823733248 | bytes 21069824 | tf_op jit(solution)/shard_map/dot_general | solution.py:13
  76.9 0.5 all-gather.12.cloned.1.call-update
  77.5 0.5 all-gather.10.cloned.1.call-update
  78.1 9.5 %convolution_convert_fusion.3 = bf16[192,4096]{1,0:T(8,128)(2,1)} fusion(bf16[192,1792]{1,0:T(8,128)(2,1)S(1)} %copy-done.5, bf16[1792,4096]{1,0:T(8,128)(2,1)} %param.10), kind=kOutput, calls=%fused_computation.5 | convolution fusion | flops 2819358720 | bytes 16941056 | tf_op jit(solution)/shard_map/dot_general | solution.py:39
  87.6 1.4 copy-done.3
  89.0 0.1 slice_bitcast_fusion.3
  89.1 1.3 pad_maximum_fusion
  90.5 3.7 %all-to-all-start.1 = ((bf16[4,192,1024]{2,1,0:T(8,128)(2,1)}), bf16[4,192,1024]{2,1,0:T(8,128)(2,1)S(1)}, u32[]{:S(2)}, u32[]{:S(2)}) async-start(bf16[4,192,1024]{2,1,0:T(8,128)(2,1)} %pad_maximum_fusion), calls=%async_computation.3 | async-start | bytes 3145728 | tf_op jit(solution)/shard_map/all_to_all | solution.py:61
  94.2 1.3 copy.17
  95.5 12.2 %fusion.12 = f32[192,4096]{1,0:T(8,128)} fusion(bf16[192,1792]{1,0:T(8,128)(2,1)S(1)} %copy-done.4, bf16[4096,1792]{1,0:T(8,128)(2,1)} %param.8), kind=kOutput, calls=%fused_computation.30 | convolution fusion | flops 2818572288 | bytes 18513920 | tf_op jit(solution)/shard_map/dot_general | solution.py:13
  107.7 19.1 %all-to-all-done.1 = bf16[4,192,1024]{2,1,0:T(8,128)(2,1)S(1)} async-done(((bf16[4,192,1024]{2,1,0:T(8,128)(2,1)}), bf16[4,192,1024]{2,1,0:T(8,128)(2,1)S(1)}, u32[]{:S(2)}, u32[]{:S(2)}) %all-to-all-start.1) | async-done | bytes 1572896 | tf_op jit(solution)/shard_map/all_to_all | solution.py:61
  126.9 3.6 %all-to-all-start = ((bf16[192,4,1024]{2,0,1:T(8,128)(2,1)}), bf16[192,4,1024]{2,0,1:T(8,128)(2,1)S(1)}, u32[]{:S(2)}, u32[]{:S(2)}) async-start(bf16[192,4,1024]{2,0,1:T(8,128)(2,1)} %bitcast.39), calls=%async_computation.2 | async-start | bytes 3145728 | tf_op jit(solution)/shard_map/all_to_all | solution.py:59
  130.5 12.8 %fusion = bf16[192,4096]{1,0:T(8,128)(2,1)} fusion(f32[192,4096]{1,0:T(8,128)} %fusion.12, bf16[192,1792]{1,0:T(8,128)(2,1)} %get-tuple-element.5, bf16[4096,1792]{1,0:T(8,128)(2,1)} %param.9), kind=kOutput, calls=%fused_computation.4 | convolution fusion | flops 2820145152 | bytes 20086784 | tf_op jit(solution)/shard_map/dot_general | solution.py:13
  143.3 9.2 %convolution_convert_fusion = bf16[4,1792,1024]{2,1,0:T(8,128)(2,1)} fusion(bf16[4,192,1792]{2,1,0:T(8,128)(2,1)} %bitcast.42, bf16[4,192,1024]{2,1,0:T(8,128)(2,1)S(1)} %all-to-all-done.1), kind=kOutput, calls=%fused_computation | convolution fusion | flops 2825912320 | bytes 19005440 | tf_op jit(solution)/shard_map/jrf,jrd->jfd/dot_general | solution.py:19
  152.6 2.7 all-to-all-done
  155.3 19.8 %all-gather.12.cloned.1.call-done = bf16[768,1792]{1,0:T(8,128)(2,1)} async-done(((bf16[192,1792]{1,0:T(8,128)(2,1)}), bf16[768,1792]{1,0:T(8,128)(2,1)}) %all-gather.12.cloned.1.call-update) | async-done | bytes 2752528 | tf_op jit(solution)/shard_map/all_gather | solution.py:70
  175.1 9.2 %convolution_convert_fusion.1 = bf16[4,1024,1792]{2,1,0:T(8,128)(2,1)} fusion(bf16[4,192,1792]{2,1,0:T(8,128)(2,1)} %bitcast.40, bf16[192,4,1024]{2,0,1:T(8,128)(2,1)S(1)} %all-to-all-done), kind=kOutput, calls=%fused_computation.1 | convolution fusion | flops 2825912320 | bytes 19005440 | tf_op jit(solution)/shard_map/jrd,jrf->jdf/dot_general | solution.py:19
  184.3 11.1 %reduce_sum.38 = bf16[1792,1024]{1,0:T(8,128)(2,1)} reduce(bf16[4,1792,1024]{2,1,0:T(8,128)(2,1)} %convolution_convert_fusion, bf16[]{:T(256)} %constant.15.clone.1), dimensions={0}, to_apply=%region_5.6 | reduce | flops 5505024 | bytes 18350082 | tf_op jit(solution)/shard_map/reduce_sum | solution.py:23
  195.5 10.9 %reduce_sum.37 = bf16[1024,1792]{1,0:T(8,128)(2,1)} reduce(bf16[4,1024,1792]{2,1,0:T(8,128)(2,1)} %convolution_convert_fusion.1, bf16[]{:T(256)} %constant.15.clone.1), dimensions={0}, to_apply=%region_4.5 | reduce | flops 5505024 | bytes 18350082 | tf_op jit(solution)/shard_map/reduce_sum | solution.py:23
  206.4 11.0 %all-gather.10.cloned.1.call-done = bf16[768,1792]{1,0:T(8,128)(2,1)} async-done(((bf16[192,1792]{1,0:T(8,128)(2,1)}), bf16[768,1792]{1,0:T(8,128)(2,1)}) %all-gather.10.cloned.1.call-update) | async-done | bytes 2752528 | tf_op jit(solution)/shard_map/all_gather | solution.py:69
  217.4 9.2 %convolution_convert_fusion.2 = bf16[4,1024,1792]{2,1,0:T(8,128)(2,1)} fusion(bf16[4,192,1792]{2,1,0:T(8,128)(2,1)} %bitcast.41, bf16[192,4,1024]{2,0,1:T(8,128)(2,1)S(1)} %all-to-all-done), kind=kOutput, calls=%fused_computation.2 | convolution fusion | flops 2825912320 | bytes 19005440 | tf_op jit(solution)/shard_map/jrd,jrf->jdf/dot_general | solution.py:19
  226.6 10.7 %reduce_sum.36 = bf16[1024,1792]{1,0:T(8,128)(2,1)} reduce(bf16[4,1024,1792]{2,1,0:T(8,128)(2,1)} %convolution_convert_fusion.2, bf16[]{:T(256)} %constant.15.clone.1), dimensions={0}, to_apply=%region_3.4 | reduce | flops 5505024 | bytes 18350082 | tf_op jit(solution)/shard_map/reduce_sum | solution.py:23
  237.3 17.0 %reduce-scatter.3.cloned.1.call-done = bf16[24,4096]{1,0:T(8,128)(2,1)} async-done(((bf16[192,4096]{1,0:T(8,128)(2,1)}), bf16[24,4096]{1,0:T(8,128)(2,1)}) %reduce-scatter.3.cloned.1.call-update) | async-done | bytes 196624 | tf_op jit(solution)/shard_map/reduce_scatter | solution.py:38
  254.3 35.5 %reduce-scatter.5.cloned.1.call-done = bf16[24,4096]{1,0:T(8,128)(2,1)} async-done(((bf16[192,4096]{1,0:T(8,128)(2,1)}), bf16[24,4096]{1,0:T(8,128)(2,1)}) %reduce-scatter.5.cloned.1.call-update) | async-done | bytes 196624 | tf_op jit(solution)/shard_map/reduce_scatter | solution.py:48
  (27 shorter events, 0.6 us)
Async XLA Ops:
  7.2 1.0 copy-start
  7.2 31.0 %all-gather.6.cloned.1.call-start = ((), (), s32[]{:S(2)}) async-start(), calls=%async_computation.4 | async-start | bytes 1769472 | tf_op jit(solution)/shard_map/all_gather | solution.py:33
  9.1 55.2 %all-gather.8.cloned.1.call-start = ((), (), s32[]{:S(2)}) async-start(), calls=%async_computation.6 | async-start | bytes 1769472 | tf_op jit(solution)/shard_map/all_gather | solution.py:44
  9.8 133.5 %all-gather.14.cloned.1.call-start = ((), (), s32[]{:S(2)}) async-start(), calls=%async_computation.10 | async-start | bytes 3440640 | tf_op jit(solution)/shard_map/all_gather | solution.py:68
  38.2 9.3 %copy-start.2 = (bf16[192,4096]{1,0:T(8,128)(2,1)S(1)}, bf16[192,4096]{1,0:T(8,128)(2,1)}, u32[]{:S(2)}) copy-start(bf16[192,4096]{1,0:T(8,128)(2,1)} %all-gather.6.cloned.1.call-done) | copy-start | bytes 4718596
  38.2 10.6 %copy-start.6 = (bf16[4096,1792]{1,0:T(8,128)(2,1)S(1)}, bf16[4096,1792]{1,0:T(8,128)(2,1)}, u32[]{:S(2)}) copy-start(bf16[4096,1792]{1,0:T(8,128)(2,1)} %param.8) | copy-start | bytes 44040196
  76.8 1.2 copy-start.5
  76.8 98.2 %all-gather.12.cloned.1.call-start = ((), (), s32[]{:S(2)}) async-start(), calls=%async_computation.9 | async-start | bytes 3440640 | tf_op jit(solution)/shard_map/all_gather | solution.py:70
  77.4 140.0 %all-gather.10.cloned.1.call-start = ((), (), s32[]{:S(2)}) async-start(), calls=%async_computation.8 | async-start | bytes 3440640 | tf_op jit(solution)/shard_map/all_gather | solution.py:69
  78.0 176.2 %reduce-scatter.3.cloned.1.call-start = ((), (), s32[]{:S(2)}) async-start(), calls=%async_computation.5 | async-start | bytes 1769472 | tf_op jit(solution)/shard_map/reduce_scatter | solution.py:38
  87.6 1.4 copy-start.3
  90.5 36.4 %all-to-all-start.1 = ((bf16[4,192,1024]{2,1,0:T(8,128)(2,1)}), bf16[4,192,1024]{2,1,0:T(8,128)(2,1)S(1)}, u32[]{:S(2)}, u32[]{:S(2)}) async-start(bf16[4,192,1024]{2,1,0:T(8,128)(2,1)} %pad_maximum_fusion), calls=%async_computation.3 | async-start | bytes 3145728 | tf_op jit(solution)/shard_map/all_to_all | solution.py:61
  94.2 1.3 copy-start.4
  126.9 28.4 %all-to-all-start = ((bf16[192,4,1024]{2,0,1:T(8,128)(2,1)}), bf16[192,4,1024]{2,0,1:T(8,128)(2,1)S(1)}, u32[]{:S(2)}, u32[]{:S(2)}) async-start(bf16[192,4,1024]{2,0,1:T(8,128)(2,1)} %bitcast.39), calls=%async_computation.2 | async-start | bytes 3145728 | tf_op jit(solution)/shard_map/all_to_all | solution.py:59
  130.4 159.3 %reduce-scatter.5.cloned.1.call-start = ((), (), s32[]{:S(2)}) async-start(), calls=%async_computation.7 | async-start | bytes 1769472 | tf_op jit(solution)/shard_map/reduce_scatter | solution.py:48
  226.6 63.2 %copy-start.1 = (bf16[32,4096]{1,0:T(8,128)(2,1)S(1)}, bf16[32,4096]{1,0:T(8,128)(2,1)}, u32[]{:S(2)}) copy-start(bf16[32,4096]{1,0:T(8,128)(2,1)} %param.6) | copy-start | bytes 786436
Sparse Core Ops, SparseCore 0:
  10.2 27.9 all-gather.5
  39.9 24.3 all-gather.7
  77.0 51.9 all-gather.13
  130.6 44.4 all-gather.11
  176.8 40.5 all-gather.9
  220.1 34.0 reduce-scatter.2
  257.1 32.5 reduce-scatter.4
